TPU v7x, 128 devices: a whole 4x4x4 slice. The times are simulated.
128 devices in a mesh: leaf: 8 (over y_lo, z), front: 16 (over x, y_hi, core).
Axes of the slice: x: 4, y: 4 (y_hi: 2, y_lo: 2; y = y_hi * 2 + y_lo), z: 4, core: 2. Of those that a mesh axis runs over, the one named last changes fastest.
Arguments:
- leaf_fronts: float32 [32768, 4096], P('leaf', 'front'), as said below
- root_front: float32 [4096, 16, 256], P(None, 'front', 'leaf'), as said below
- leaf_order: int32 [8, 16], P('leaf'), may hold values from 0 to 15, each once within a row
- leaf_map: int32 [8, 16], P('leaf'), may hold values from 0 to 15, each once within a row
- root_order: int32 [16], replicated, may hold values from 0 to 15, each once
Outputs:
- leaf_factor: float32 [32768, 4096], P('leaf', 'front')
- root_factor: float32 [4096, 16, 256], P(None, 'front', 'leaf')
Inputs may be any that keep to these rules, and one draw needn't show every extreme that they name: `leaf_fronts`: each leaf block of 4096 rows is symmetric and positive definite. `root_front`: symmetric and positive definite. `leaf_order`: each row names every block column once. `leaf_map`: each row names every root block once. `root_order`: names every block column once.
All inputs are finite; a program needn't handle non-finite values.
Results may differ from a plain program's by a relative error of at most 0.00018.
Values sent between devices are 32-bit elements; how exact they have to be, the bound alone decides.
A program may use at most 128 MiB of HBM per device.

v0:
```python
import jax
import jax.numpy as jnp
from jax import lax
from jax.sharding import PartitionSpec as P

HIGH = lax.Precision.HIGH


def invert(permutation):
    block_ids = jnp.arange(permutation.shape[0], dtype=jnp.int32)
    hits = permutation[None, :] == block_ids[:, None]
    return jnp.sum(jnp.where(hits, block_ids[None, :], 0), axis=1)


def make_panel(raw_column, pivot_block, alive_set):
    block_size = raw_column.shape[1]
    block_count = raw_column.shape[0] // block_size
    diag_block = lax.dynamic_slice_in_dim(raw_column, pivot_block * block_size, block_size, 0)
    lower = jnp.linalg.cholesky(diag_block)
    solved = lax.linalg.triangular_solve(
        lower, raw_column, left_side=False, lower=True, transpose_a=True
    )
    block_ids = jnp.arange(block_count, dtype=jnp.int32)
    keep = (alive_set & (block_ids != pivot_block))[:, None, None]
    tiles = solved.reshape(block_count, block_size, block_size)
    on_pivot = (block_ids == pivot_block)[:, None, None]
    tiles = jnp.where(on_pivot, lower[None], jnp.where(keep, tiles, 0.0))
    return tiles.reshape(block_count * block_size, block_size)


def block_row(tiles, pivot_block):
    return lax.dynamic_index_in_dim(tiles, pivot_block, 0, keepdims=False)


def shards(leaf_fronts, root_front, leaf_order, leaf_map, root_order):
    order_rows, block_size = leaf_fronts.shape
    block_count = order_rows // block_size
    my_block = lax.axis_index("front")
    leaf_index = lax.axis_index("leaf")
    slice_width = root_front.shape[2]
    block_ids = jnp.arange(block_count, dtype=jnp.int32)
    own_start = my_block * block_size
    tiles = leaf_fronts.reshape(block_count, block_size, block_size)
    first, second = (leaf_order[0, 0], leaf_order[0, 1])
    raw_first = lax.all_gather(block_row(tiles, first).T, "front", axis=0, tiled=True)
    raw_second = lax.all_gather(block_row(tiles, second).T, "front", axis=0, tiled=True)
    everything = jnp.ones((block_count,), dtype=jnp.bool_)
    panel_first = make_panel(raw_first, first, everything)
    alive = block_ids != first
    pivot_rows = lax.dynamic_slice_in_dim(panel_first, second * block_size, block_size, 0)
    raw_second = raw_second - jnp.dot(panel_first, pivot_rows.T, precision=HIGH)
    panel_second = make_panel(raw_second, second, alive)
    alive = alive & (block_ids != second)
    own_first = lax.dynamic_slice_in_dim(panel_first, own_start, block_size, 0)
    own_second = lax.dynamic_slice_in_dim(panel_second, own_start, block_size, 0)
    updated = (
        leaf_fronts
        - jnp.dot(panel_first, own_first.T, precision=HIGH)
        - jnp.dot(panel_second, own_second.T, precision=HIGH)
    )
    updated = updated.reshape(block_count, block_size, block_size)
    updated = jnp.where(alive[:, None, None], updated, 0.0)
    leaf_out = jnp.where(
        my_block == first,
        panel_first,
        jnp.where(my_block == second, panel_second, updated.reshape(order_rows, block_size)),
    )
    mine_alive = alive[my_block]
    inverse = invert(leaf_map[0])
    outgoing = jnp.take(jnp.where(mine_alive, updated, 0.0), inverse, axis=0)
    incoming = lax.all_to_all(outgoing, "front", split_axis=0, concat_axis=0, tiled=True)
    gathered = jnp.swapaxes(jnp.take(incoming, inverse, axis=0), 0, 1)
    gathered = gathered.reshape(block_size, order_rows)
    part = lax.psum_scatter(gathered, "leaf", scatter_dimension=0, tiled=True)
    part = part + root_front[:, 0, :].T
    pivot = root_order[0]
    row = lax.dynamic_slice_in_dim(part, pivot * block_size, block_size, 1)
    raw_root = lax.all_gather(row, ("front", "leaf"), axis=0, tiled=True)
    panel = make_panel(raw_root, pivot, everything)
    own = lax.dynamic_slice_in_dim(panel, own_start + leaf_index * slice_width, slice_width, 0)
    part = part - jnp.dot(own, panel.T, precision=HIGH)
    part = part.reshape(slice_width, block_count, block_size)
    part = jnp.where((block_ids != pivot)[None, :, None], part, 0.0)
    part = part.reshape(slice_width, order_rows)
    own_panel = lax.dynamic_slice_in_dim(panel, leaf_index * slice_width, slice_width, 1)
    root_out = jnp.where(my_block == pivot, own_panel, part.T)
    return (leaf_out, root_out[:, None, :])


def solution(mesh):
    return jax.shard_map(
        shards,
        mesh=mesh,
        in_specs=(
            P("leaf", "front"),
            P(None, "front", "leaf"),
            P("leaf", None),
            P("leaf", None),
            P(),
        ),
        out_specs=(P("leaf", "front"), P(None, "front", "leaf")),
        check_vma=False,
    )
```

profile of v0, /device:TPU:1, one launch (start us, length us, event | category | flops | bytes accessed | tf_op | source)
XLA Modules:
  0.0 781.4 jit_solution(6167048104012507612)
XLA Ops:
  7.2 1.3 fusion.45
  11.8 1.9 dynamic-slice_bitcast_fusion
  16.7 5.6 copy.75
  22.9 1.1 compare_and_fusion.1
  25.0 51.5 %all-gather.4.cloned.1.call-done = f32[4096,256]{0,1:T(8,128)} async-done(((f32[256,256]{0,1:T(8,128)}), f32[4096,256]{0,1:T(8,128)}) %all-gather.4.cloned.1.call-update) | async-done | bytes 4194320 | tf_op jit(solution)/shard_map/all_gather | solution.py:45
  76.5 1.0 constant_dynamic-slice_fusion.6
  77.6 1.0 fusion.15
  78.7 11.7 %cholesky.172 = f32[128,128]{1,0:T(8,128)S(1)} custom-call(f32[128,128]{1,0:T(8,128)S(1)} %cholesky.270), custom_call_target="Cholesky" | custom-call | tf_op jit(solution)/shard_map/jit(cholesky)/cholesky | solution.py:19
  90.4 9.8 %custom-call.15 = f32[1,128,128]{1,2,0:T(8,128)S(1)} custom-call(f32[1,128,128]{2,1,0:T(8,128)S(1)} %get-tuple-element.87), custom_call_target="InvertDiagBlocksLowerTriangular" | custom-call | tf_op jit(solution)/shard_map/jit(cholesky)/cholesky | solution.py:19
  100.7 11.7 %cholesky.189 = f32[128,128]{1,0:T(8,128)S(1)} custom-call(f32[128,128]{1,0:T(8,128)S(1)} %convolution_subtract_fusion.9), custom_call_target="Cholesky" | custom-call | tf_op jit(solution)/shard_map/jit(cholesky)/cholesky | solution.py:19
  114.6 3.8 while.6
  115.2 1.3 bitcast_dynamic-update-slice_fusion.6
  117.1 1.3 bitcast_dynamic-update-slice_fusion.6
  118.4 20.0 %custom-call.16 = f32[2,128,128]{1,2,0:T(8,128)S(1)} custom-call(f32[2,128,128]{2,1,0:T(8,128)S(1)} %get-tuple-element.25), custom_call_target="InvertDiagBlocksLowerTriangular" | custom-call | tf_op jit(solution)/shard_map/triangular_solve/custom-call.0 | solution.py:20
  138.8 3.9 copy.94
  142.6 1.9 fusion.11
  144.6 2.1 convolution_subtract_fusion.5
  146.6 2.0 fusion.31
  148.6 2.8 fusion.4
  151.5 5.7 convolution_subtract_fusion.2
  157.2 2.0 copy-done.1
  159.3 1.0 fusion.14
  160.3 11.7 %cholesky.206 = f32[128,128]{1,0:T(8,128)S(1)} custom-call(f32[128,128]{1,0:T(8,128)S(1)} %cholesky.273), custom_call_target="Cholesky" | custom-call | tf_op jit(solution)/shard_map/jit(cholesky)/cholesky | solution.py:19
  172.7 9.8 %custom-call.17 = f32[1,128,128]{1,2,0:T(8,128)S(1)} custom-call(f32[1,128,128]{2,1,0:T(8,128)S(1)} %get-tuple-element.83), custom_call_target="InvertDiagBlocksLowerTriangular" | custom-call | tf_op jit(solution)/shard_map/jit(cholesky)/cholesky | solution.py:19
  183.0 11.7 %cholesky.223 = f32[128,128]{1,0:T(8,128)S(1)} custom-call(f32[128,128]{1,0:T(8,128)S(1)} %convolution_subtract_fusion.8), custom_call_target="Cholesky" | custom-call | tf_op jit(solution)/shard_map/jit(cholesky)/cholesky | solution.py:19
  197.0 4.1 while.7
  197.6 1.4 bitcast_dynamic-update-slice_fusion.7
  199.6 1.4 bitcast_dynamic-update-slice_fusion.7
  201.1 20.1 %custom-call.18 = f32[2,128,128]{1,2,0:T(8,128)S(1)} custom-call(f32[2,128,128]{2,1,0:T(8,128)S(1)} %get-tuple-element.26), custom_call_target="InvertDiagBlocksLowerTriangular" | custom-call | tf_op jit(solution)/shard_map/triangular_solve/custom-call.0 | solution.py:20
  221.2 3.6 fusion.9
  224.8 2.0 convolution_subtract_fusion.4
  226.8 2.0 fusion.27
  229.2 3.9 copy.95
  233.1 2.2 convolution_subtract_fusion.1
  235.3 0.8 fusion.5
  236.1 6.2 select_select_fusion.1
  242.3 5.6 copy.90
  247.9 5.3 select_select_fusion
  253.2 4.9 gather_fusion
  258.1 2.8 broadcast_select_fusion
  260.9 54.1 %all_to_all.5 = f32[16,256,256]{2,1,0:T(8,128)} all-to-all(f32[16,256,256]{2,1,0:T(8,128)S(1)} %broadcast_select_fusion), channel_id=1, replica_groups=mesh['leaf'=8,'front'=16] {'front'}, dimensions={0} | all-to-all | bytes 8388608 | tf_op jit(solution)/shard_map/all_to_all | solution.py:71
  315.1 5.0 gather_fusion.1
  320.1 4.7 select_bitcast_fusion
  324.8 5.3 copy.79
  330.1 5.6 copy.91
  336.4 51.2 %reduce-scatter.4.cloned.1.call-done = f32[32,4096]{1,0:T(8,128)} async-done(((f32[256,4096]{1,0:T(8,128)}), f32[32,4096]{1,0:T(8,128)}) %reduce-scatter.4.cloned.1.call-update) | async-done | bytes 524304 | tf_op jit(solution)/shard_map/reduce_scatter | solution.py:74
  387.6 1.1 bitcast_add_fusion
  389.6 5.6 copy.84
  395.2 300.0 %all-gather.8.cloned.1.call-done = f32[4096,256]{1,0:T(8,128)} async-done(((f32[32,256]{1,0:T(8,128)}), f32[4096,256]{1,0:T(8,128)}) %all-gather.8.cloned.1.call-update) | async-done | bytes 4194320 | tf_op jit(solution)/shard_map/all_gather | solution.py:78
  695.2 1.0 constant_dynamic-slice_fusion.3
  696.3 1.0 fusion.13
  697.4 11.7 %cholesky.240 = f32[128,128]{1,0:T(8,128)S(1)} custom-call(f32[128,128]{1,0:T(8,128)S(1)} %cholesky.276), custom_call_target="Cholesky" | custom-call | tf_op jit(solution)/shard_map/jit(cholesky)/cholesky | solution.py:19
  709.7 9.8 %custom-call.19 = f32[1,128,128]{1,2,0:T(8,128)S(1)} custom-call(f32[1,128,128]{2,1,0:T(8,128)S(1)} %get-tuple-element.79), custom_call_target="InvertDiagBlocksLowerTriangular" | custom-call | tf_op jit(solution)/shard_map/jit(cholesky)/cholesky | solution.py:19
  720.1 11.7 %cholesky.257 = f32[128,128]{1,0:T(8,128)S(1)} custom-call(f32[128,128]{1,0:T(8,128)S(1)} %convolution_subtract_fusion.7), custom_call_target="Cholesky" | custom-call | tf_op jit(solution)/shard_map/jit(cholesky)/cholesky | solution.py:19
  734.1 4.1 while.8
  734.7 1.4 bitcast_dynamic-update-slice_fusion.8
  736.7 1.4 bitcast_dynamic-update-slice_fusion.8
  738.1 19.9 %custom-call.20 = f32[2,128,128]{1,2,0:T(8,128)S(1)} custom-call(f32[2,128,128]{2,1,0:T(8,128)S(1)} %get-tuple-element.27), custom_call_target="InvertDiagBlocksLowerTriangular" | custom-call | tf_op jit(solution)/shard_map/triangular_solve/custom-call.0 | solution.py:20
  758.0 3.7 fusion.7
  761.7 3.5 convolution_subtract_fusion.3
  765.3 2.0 fusion.23
  767.6 3.8 copy.96
  771.4 0.8 fusion.6
  772.2 2.2 fusion.3
  (99 shorter events, 14.6 us)
Async XLA Ops:
  7.2 69.4 %all-gather.4.cloned.1.call-start = ((), (), s32[]{:S(2)}) async-start(), calls=%async_computation.2 | async-start | bytes 4456448 | tf_op jit(solution)/shard_map/all_gather | solution.py:45
  13.6 137.8 %all-gather.6.cloned.1.call-start = ((), (), s32[]{:S(2)}) async-start(), calls=%async_computation.3 | async-start | bytes 4456448 | tf_op jit(solution)/shard_map/all_gather | solution.py:46
  14.4 373.2 %reduce-scatter.4.cloned.1.call-start = ((), (), s32[]{:S(2)}) async-start(), calls=%async_computation.5 | async-start | bytes 4718592 | tf_op jit(solution)/shard_map/reduce_scatter | solution.py:74
  16.6 8.2 %copy-start.7 = (s32[1,16]{1,0:T(1,128)S(1)}, s32[1,16]{1,0:T(1,128)}, u32[]{:S(2)}) copy-start(s32[1,16]{1,0:T(1,128)} %param.13) | copy-start | bytes 196
  138.8 3.9 copy-start.4
  157.2 2.0 copy-start.1
  221.1 3.7 copy-start.2
  229.2 3.9 copy-start
  229.2 3.9 copy-start.3
  335.7 0.7 copy-start.8
  335.7 51.9 %copy-start.6 = (f32[4096,1,32]{0,2,1:T(8,128)S(1)}, f32[4096,1,32]{0,2,1:T(8,128)}, u32[]{:S(2)}) copy-start(f32[4096,1,32]{0,2,1:T(8,128)} %param.11) | copy-start | bytes 1572868
  335.7 359.5 %all-gather.8.cloned.1.call-start = ((), (), s32[]{:S(2)}) async-start(), calls=%async_computation.4 | async-start | bytes 4227072 | tf_op jit(solution)/shard_map/all_gather | solution.py:78
  758.0 3.7 copy-start.5
Sparse Core Ops, SparseCore 0:
  13.8 62.7 all-gather.3
  79.4 58.3 all-gather.5
  335.9 51.7 reduce-scatter.3
  389.7 305.4 all-gather.7
where the time goes:
time: 792 us; the launch traced here: 781 us
  waiting for transfers between devices  403 us (51%)
  other arithmetic  187 us (24%)
  local copies, waits for them, and re-layouts  72.4 us (9%)
  blocking collectives  54.1 us (7%)
  matrix products  40.5 us (5%)
  between operations  24.1 us (3%)
    all_gather x1, waiting for transfers between devices, shards(): raw_root = lax.all_gather(row, ('front', 'leaf'), axis=0, tiled=True)  300 us
    another operation x20, other arithmetic, make_panel(): lower = jnp.linalg.cholesky(diag_block)  103 us
    another operation x7, other arithmetic, make_panel(): lax.linalg.triangular_solve(lower, raw_column, left_side=False, lower=Tru...  60.1 us
    all_to_all x1, blocking collectives, shards(): lax.all_to_all(outgoing, 'front', split_axis=0, concat_axis=0, tiled=True)  54.1 us
    all_gather x1, waiting for transfers between devices, shards(): lax.all_gather(block_row(tiles, first).T, 'front', axis=0, tiled=True)  51.5 us
    reduce_scatter x1, waiting for transfers between devices, shards(): part = lax.psum_scatter(gathered, 'leaf', scatter_dimension=0, tiled=True)  51.2 us
    unnamed x25, local copies, waits for them, and re-layouts  31.1 us
    another operation x9, matrix products, make_panel(): lax.linalg.triangular_solve(lower, raw_column, left_side=False, lower=Tru...  22.8 us
  transfers between devices with their start and end apart: 4, of which 3 were waited for; matrix products, arithmetic and copies ran while one was open for 11% of the time, Pallas kernels for 0%

commit v1 on v0

--- a/solution.py
+++ b/solution.py
@@ -75,7 +75,10 @@
     part = part + root_front[:, 0, :].T
     pivot = root_order[0]
     row = lax.dynamic_slice_in_dim(part, pivot * block_size, block_size, 1)
-    raw_root = lax.all_gather(row, ("front", "leaf"), axis=0, tiled=True)
+    big = jax.lax.axis_size(("front", "leaf"))
+    moved = jnp.stack([row] * big)
+    v_now = jax.lax.all_to_all(moved, ("front", "leaf"), 0, 0)
+    raw_root = jnp.concatenate(v_now, 0)
     panel = make_panel(raw_root, pivot, everything)
     own = lax.dynamic_slice_in_dim(panel, own_start + leaf_index * slice_width, slice_width, 0)
     part = part - jnp.dot(own, panel.T, precision=HIGH)

time: 792 us -> 540 us (0.68)
  waiting for transfers between devices: 403 us -> 149 us
    all_gather x1 -> x0, waiting for transfers between devices: 300 us -> none  [shards(): raw_root = lax.all_gather(row, ('front', 'leaf'), axis=0, tiled=True)]
    all_to_all x0 -> x1, waiting for transfers between devices: none -> 46.2 us  [shards(): v_now = jax.lax.all_to_all(moved, ('front', 'leaf'), 0, 0)]
    unnamed x25 -> x22, local copies, waits for them, and re-layouts: 31.1 us -> 25.5 us
  transfers between devices with their start and end apart: 4 -> 4, of which waited for: 3 -> 3; matrix products, arithmetic and copies ran while one was open for 11% -> 17% of each run, Pallas kernels for 0% -> 0%
where the time goes in v1:
time: 540 us; the launch traced here: 529 us
  other arithmetic  185 us (34%)
  waiting for transfers between devices  149 us (28%)
  local copies, waits for them, and re-layouts  66 us (12%)
  blocking collectives  54.1 us (10%)
  matrix products  42.2 us (8%)
  between operations  25.2 us (5%)
  starting transfers between devices  7.84 us (1%)
    another operation x20, other arithmetic, make_panel(): lower = jnp.linalg.cholesky(diag_block)  103 us
    another operation x7, other arithmetic, make_panel(): lax.linalg.triangular_solve(lower, raw_column, left_side=False, lower=Tru...  59.9 us
    all_to_all x1, blocking collectives, shards(): lax.all_to_all(outgoing, 'front', split_axis=0, concat_axis=0, tiled=True)  54.1 us
    reduce_scatter x1, waiting for transfers between devices, shards(): part = lax.psum_scatter(gathered, 'leaf', scatter_dimension=0, tiled=True)  51.2 us
    all_gather x1, waiting for transfers between devices, shards(): lax.all_gather(block_row(tiles, first).T, 'front', axis=0, tiled=True)  50.6 us
    all_to_all x1, waiting for transfers between devices, shards(): v_now = jax.lax.all_to_all(moved, ('front', 'leaf'), 0, 0)  46.2 us
    unnamed x22, local copies, waits for them, and re-layouts  25.5 us
    another operation x9, matrix products, make_panel(): lax.linalg.triangular_solve(lower, raw_column, left_side=False, lower=Tru...  24.3 us
  transfers between devices with their start and end apart: 4, of which 3 were waited for; matrix products, arithmetic and copies ran while one was open for 17% of the time, Pallas kernels for 0%

profile of v1, /device:TPU:1, one launch (start us, length us, event | category | flops | bytes accessed | tf_op | source)
XLA Modules:
  0.0 529.0 jit_solution(10848821269463079468)
XLA Ops:
  7.2 1.3 fusion.45
  12.5 1.9 dynamic-slice_bitcast_fusion
  17.8 5.6 %copy.40 = f32[4096,256]{0,1:T(8,128)} copy(f32[4096,256]{1,0:T(8,128)} %param.10) | data formatting | bytes 8388608 | tf_op args[0]
  24.2 1.3 compare_and_fusion.1
  26.6 50.6 %all-gather.3.cloned.1.call-done = f32[4096,256]{0,1:T(8,128)} async-done(((f32[256,256]{0,1:T(8,128)}), f32[4096,256]{0,1:T(8,128)}) %all-gather.3.cloned.1.call-update) | async-done | bytes 4194320 | tf_op jit(solution)/shard_map/all_gather | solution.py:45
  77.2 1.0 constant_dynamic-slice_fusion.6
  78.4 1.0 fusion.15
  79.4 11.7 %cholesky.172 = f32[128,128]{1,0:T(8,128)S(1)} custom-call(f32[128,128]{1,0:T(8,128)S(1)} %cholesky.270), custom_call_target="Cholesky" | custom-call | tf_op jit(solution)/shard_map/jit(cholesky)/cholesky | solution.py:19
  91.1 9.8 %custom-call.15 = f32[1,128,128]{1,2,0:T(8,128)S(1)} custom-call(f32[1,128,128]{2,1,0:T(8,128)S(1)} %get-tuple-element.83), custom_call_target="InvertDiagBlocksLowerTriangular" | custom-call | tf_op jit(solution)/shard_map/jit(cholesky)/cholesky | solution.py:19
  101.4 11.7 %cholesky.189 = f32[128,128]{1,0:T(8,128)S(1)} custom-call(f32[128,128]{1,0:T(8,128)S(1)} %convolution_subtract_fusion.9), custom_call_target="Cholesky" | custom-call | tf_op jit(solution)/shard_map/jit(cholesky)/cholesky | solution.py:19
  115.5 4.1 while.6
  116.1 1.4 bitcast_dynamic-update-slice_fusion.6
  118.1 1.4 bitcast_dynamic-update-slice_fusion.6
  119.6 20.0 %custom-call.16 = f32[2,128,128]{1,2,0:T(8,128)S(1)} custom-call(f32[2,128,128]{2,1,0:T(8,128)S(1)} %get-tuple-element.25), custom_call_target="InvertDiagBlocksLowerTriangular" | custom-call | tf_op jit(solution)/shard_map/triangular_solve/custom-call.0 | solution.py:20
  140.0 3.9 copy.57
  143.8 1.9 fusion.11
  145.8 2.1 convolution_subtract_fusion.5
  147.8 2.0 fusion.31
  149.8 2.8 fusion.4
  152.7 5.7 %convolution_subtract_fusion.2 = f32[4096,256]{0,1:T(8,128)S(1)} fusion(f32[4096,256]{0,1:T(8,128)} %all-gather.5.cloned.1.call-done, f32[4096,256]{0,1:T(8,128)} %fusion.4, s32[]{:T(128)S(6)} %select_n.119), kind=kOutput, calls=%fused_computation.10 | convolution fusion | flops 1611661312 | bytes 12845060 | tf_op jit(solution)/shard_map/dot_general | solution.py:51
  158.4 2.0 copy-done.1
  160.5 1.0 fusion.14
  161.5 11.7 %cholesky.206 = f32[128,128]{1,0:T(8,128)S(1)} custom-call(f32[128,128]{1,0:T(8,128)S(1)} %cholesky.273), custom_call_target="Cholesky" | custom-call | tf_op jit(solution)/shard_map/jit(cholesky)/cholesky | solution.py:19
  173.9 9.8 %custom-call.17 = f32[1,128,128]{1,2,0:T(8,128)S(1)} custom-call(f32[1,128,128]{2,1,0:T(8,128)S(1)} %get-tuple-element.79), custom_call_target="InvertDiagBlocksLowerTriangular" | custom-call | tf_op jit(solution)/shard_map/jit(cholesky)/cholesky | solution.py:19
  184.2 11.7 %cholesky.223 = f32[128,128]{1,0:T(8,128)S(1)} custom-call(f32[128,128]{1,0:T(8,128)S(1)} %convolution_subtract_fusion.8), custom_call_target="Cholesky" | custom-call | tf_op jit(solution)/shard_map/jit(cholesky)/cholesky | solution.py:19
  198.1 4.0 while.7
  198.7 1.4 bitcast_dynamic-update-slice_fusion.7
  200.7 1.4 bitcast_dynamic-update-slice_fusion.7
  202.0 19.9 %custom-call.18 = f32[2,128,128]{1,2,0:T(8,128)S(1)} custom-call(f32[2,128,128]{2,1,0:T(8,128)S(1)} %get-tuple-element.26), custom_call_target="InvertDiagBlocksLowerTriangular" | custom-call | tf_op jit(solution)/shard_map/triangular_solve/custom-call.0 | solution.py:20
  221.9 3.6 fusion.9
  225.6 2.0 convolution_subtract_fusion.4
  227.6 2.0 fusion.27
  230.0 3.9 copy.58
  233.9 2.4 convolution_subtract_fusion.1
  237.2 6.2 %select_select_fusion.1 = (f32[4096,256]{0,1:T(8,128)}, f32[4096,256]{0,1:T(8,128)}) fusion(f32[4096,256]{0,1:T(8,128)S(1)} %copy-done, f32[4096,256]{0,1:T(8,128)S(1)} %fusion.5, pred[4096]{0:T(1024)(128)(4,1)S(1)} %broadcast_in_dim.165, pred[]{:T(512)S(6)} %eq.57, pred[]{:T(512)S(6)} %eq.54, f32[4096,256]{0,1:T(8,128)S(1)} %convolution_subtract_fusion.1, ...), kind=kOutput, calls=%fused_computation.27 | convolution fusion | flops 1614807040 | bytes 25432070 | tf_op jit(solution)/shard_map/dot_general | solution.py:59
  243.3 5.6 %copy.54 = f32[4096,256]{1,0:T(8,128)} copy(f32[4096,256]{0,1:T(8,128)} %get-tuple-element.91) | data formatting | bytes 8388608 | tf_op jit(solution)/shard_map/reshape | solution.py:61
  248.9 5.4 %select_select_fusion = f32[16,256,256]{2,1,0:T(8,128)} fusion(f32[16,256,256]{2,1,0:T(8,128)} %bitcast.149, pred[16]{0:T(512)(128)(4,1)S(1)} %get-tuple-element.94, pred[]{:T(512)} %bitcast.21), kind=kLoop, calls=%fused_computation.26 | loop fusion | flops 2097152 | bytes 8388625 | tf_op jit(solution)/shard_map/jit(_where)/select_n | solution.py:70
  254.3 4.9 gather_fusion
  259.3 2.8 broadcast_select_fusion
  262.1 54.1 %all_to_all.10 = f32[16,256,256]{2,1,0:T(8,128)} all-to-all(f32[16,256,256]{2,1,0:T(8,128)S(1)} %broadcast_select_fusion), channel_id=1, replica_groups=mesh['leaf'=8,'front'=16] {'front'}, dimensions={0} | all-to-all | bytes 8388608 | tf_op jit(solution)/shard_map/all_to_all | solution.py:71
  316.2 5.0 gather_fusion.1
  321.2 2.8 select_bitcast_fusion
  324.0 2.6 copy.56
  327.3 51.2 %reduce-scatter.2.cloned.1.call-done = f32[32,4096]{1,0:T(8,128)} async-done(((f32[256,4096]{1,0:T(8,128)}), f32[32,4096]{1,0:T(8,128)}) %reduce-scatter.2.cloned.1.call-update) | async-done | bytes 524304 | tf_op jit(solution)/shard_map/reduce_scatter | solution.py:74
  378.5 1.1 bitcast_add_fusion
  379.6 2.5 stack.2
  382.1 7.7 %all-to-all-start.1 = ((f32[128,32,256]{2,1,0:T(8,128)}), f32[128,32,256]{2,1,0:T(8,128)}, u32[]{:S(2)}, u32[]{:S(2)}) async-start(f32[128,32,256]{2,1,0:T(8,128)} %stack.2), calls=%async_computation.2 | async-start | bytes 8388608 | tf_op jit(solution)/shard_map/all_to_all | solution.py:80
  390.1 5.6 %copy.48 = f32[4096,256]{1,0:T(8,128)} copy(f32[4096,256]{0,1:T(8,128)} %get-tuple-element.90) | data formatting | bytes 8388608
  395.7 46.2 %all-to-all-done.1 = f32[128,32,256]{2,1,0:T(8,128)} async-done(((f32[128,32,256]{2,1,0:T(8,128)}), f32[128,32,256]{2,1,0:T(8,128)}, u32[]{:S(2)}, u32[]{:S(2)}) %all-to-all-start.1) | async-done | bytes 4194336 | tf_op jit(solution)/shard_map/all_to_all | solution.py:80
  441.8 1.0 constant_dynamic-slice_fusion.3
  443.0 1.0 fusion.13
  444.0 11.7 %cholesky.240 = f32[128,128]{1,0:T(8,128)S(1)} custom-call(f32[128,128]{1,0:T(8,128)S(1)} %cholesky.276), custom_call_target="Cholesky" | custom-call | tf_op jit(solution)/shard_map/jit(cholesky)/cholesky | solution.py:19
  456.4 9.8 %custom-call.19 = f32[1,128,128]{1,2,0:T(8,128)S(1)} custom-call(f32[1,128,128]{2,1,0:T(8,128)S(1)} %get-tuple-element.75), custom_call_target="InvertDiagBlocksLowerTriangular" | custom-call | tf_op jit(solution)/shard_map/jit(cholesky)/cholesky | solution.py:19
  466.7 11.7 %cholesky.257 = f32[128,128]{1,0:T(8,128)S(1)} custom-call(f32[128,128]{1,0:T(8,128)S(1)} %convolution_subtract_fusion.7), custom_call_target="Cholesky" | custom-call | tf_op jit(solution)/shard_map/jit(cholesky)/cholesky | solution.py:19
  480.5 3.8 while.8
  481.1 1.3 bitcast_dynamic-update-slice_fusion.8
  483.0 1.3 bitcast_dynamic-update-slice_fusion.8
  484.3 19.9 %custom-call.20 = f32[2,128,128]{1,2,0:T(8,128)S(1)} custom-call(f32[2,128,128]{2,1,0:T(8,128)S(1)} %get-tuple-element.27), custom_call_target="InvertDiagBlocksLowerTriangular" | custom-call | tf_op jit(solution)/shard_map/triangular_solve/custom-call.0 | solution.py:20
  504.2 3.5 fusion.7
  507.7 5.1 convolution_subtract_fusion.3
  512.9 2.0 fusion.23
  515.3 3.8 copy.59
  519.1 0.8 fusion.6
  519.9 2.2 fusion.3
  (96 shorter events, 14.9 us)
Async XLA Ops:
  7.2 70.1 %all-gather.3.cloned.1.call-start = ((), (), s32[]{:S(2)}) async-start(), calls=%async_computation.3 | async-start | bytes 4456448 | tf_op jit(solution)/shard_map/all_gather | solution.py:45
  14.4 138.3 %all-gather.5.cloned.1.call-start = ((), (), s32[]{:S(2)}) async-start(), calls=%async_computation.4 | async-start | bytes 4456448 | tf_op jit(solution)/shard_map/all_gather | solution.py:46
  15.1 363.4 %reduce-scatter.2.cloned.1.call-start = ((), (), s32[]{:S(2)}) async-start(), calls=%async_computation.5 | async-start | bytes 4718592 | tf_op jit(solution)/shard_map/reduce_scatter | solution.py:74
  17.8 8.7 %copy-start.6 = (s32[1,16]{1,0:T(1,128)S(1)}, s32[1,16]{1,0:T(1,128)}, u32[]{:S(2)}) copy-start(s32[1,16]{1,0:T(1,128)} %param.13) | copy-start | bytes 196
  140.0 3.9 copy-start.4
  158.3 2.0 copy-start.1
  221.9 3.7 copy-start.2
  230.0 3.9 copy-start
  230.0 3.9 copy-start.3
  326.6 0.7 copy-start.7
  326.6 51.9 %copy-start.5 = (f32[4096,1,32]{0,2,1:T(8,128)S(1)}, f32[4096,1,32]{0,2,1:T(8,128)}, u32[]{:S(2)}) copy-start(f32[4096,1,32]{0,2,1:T(8,128)} %param.11) | copy-start | bytes 1572868
  382.1 59.8 %all-to-all-start.1 = ((f32[128,32,256]{2,1,0:T(8,128)}), f32[128,32,256]{2,1,0:T(8,128)}, u32[]{:S(2)}, u32[]{:S(2)}) async-start(f32[128,32,256]{2,1,0:T(8,128)} %stack.2), calls=%async_computation.2 | async-start | bytes 8388608 | tf_op jit(solution)/shard_map/all_to_all | solution.py:80
Sparse Core Ops, SparseCore 0:
  14.5 62.7 all-gather.2
  80.1 58.1 all-gather.4
  326.8 51.6 reduce-scatter.1
